TPU v7x, 32 devices: a whole 2x2x4 slice. The times are simulated.
32 devices in a mesh: trc: 4 (over z), lat: 4 (over x, core), lon: 2 (over y).
Axes of the slice: x: 2, y: 2, z: 4, core: 2. Of those that a mesh axis runs over, the one named last changes fastest.
Arguments:
- species_concentrations: float32 [32, 8, 128, 256], P('trc', None, 'lat', 'lon'), may hold values from 0.2 to 4
- zonal_velocity_array: float32 [8, 128, 256], P('trc', 'lat', 'lon'), may hold values from -2.5 to 2.5
- meridional_velocity_array: float32 [8, 128, 256], P('trc', 'lat', 'lon'), may hold values from -2.5 to 2.5
- thermal_anomaly: float32 [8, 128, 256], P('trc', 'lat', 'lon'), may hold values from -6 to 6
- ocean_top_height_grid: float32 [128, 256], P('lat', 'lon'), may hold values from -6 to 6
- water_layer_tally: int32 [128, 256], P('lat', 'lon'), may hold values from 0 to 8
- species_interaction_table: float32 [32, 32], replicated, may hold values from -1 to 1
- species_production_pace: float32 [32], replicated, may hold values from 0.2 to 2
- photon_uptake: float32 [32], replicated, may hold values from 0.01 to 0.1
Outputs:
- updated_tracers: float32 [32, 8, 128, 256], P('trc', None, 'lat', 'lon')
- east_out: float32 [8, 128, 256], P('trc', 'lat', 'lon')
- north_out: float32 [8, 128, 256], P('trc', 'lat', 'lon')
- temperature_out: float32 [8, 128, 256], P('trc', 'lat', 'lon')
- height_out: float32 [128, 256], P('lat', 'lon')
Inputs may be any that keep to these rules, and one draw needn't show every extreme that they name: `water_layer_tally`: the number of wet levels of a column, counted from the surface; cells below it, and whole columns with 0, are land.
All inputs are finite; a program needn't handle non-finite values.
Results may differ from a plain program's by a relative error of at most 0.0003.
Values sent between devices are 32-bit elements; how exact they have to be, the bound alone decides.
No kernel may reach another device: no remote copies, remote signals or barrier semaphores. Data moves between devices by JAX's collectives and lax.ppermute only.
A program may use at most 64 MiB of HBM per device.

v0:
```python
import math
import jax
import jax.numpy as jnp
from jax import lax
from jax.sharding import PartitionSpec as P

HIGHEST = lax.Precision.HIGHEST
TIME_STEP = 0.1
GRAVITY = 1.0
VISCOSITY = 0.2
BOTTOM_DRAG = 0.05
DEPTH_SCALE = 0.5
CORIOLIS_SCALE = 0.5
COLUMN_DEPTH = 2.0
WATER_ABSORB = 0.2
HALF_LIGHT = 0.5
REACT_STEP = 0.1
WARMING_WEIGHT = 1.0


def padded(block, sides, width, periodic):
    for axis, dim in sides:
        count = lax.axis_size(axis)
        forward = [(i, i + 1) for i in range(count - 1)]
        if periodic:
            forward.append((count - 1, 0))
        backward = [(target, source) for source, target in forward]
        low = lax.ppermute(
            lax.slice_in_dim(block, block.shape[dim] - width, None, axis=dim), axis, forward
        )
        high = lax.ppermute(lax.slice_in_dim(block, 0, width, axis=dim), axis, backward)
        block = jnp.concatenate([low, block, high], axis=dim)
    return block


def limited_slope(ahead, behind):
    smaller = jnp.minimum(jnp.abs(ahead), jnp.abs(behind))
    return jnp.where(
        ahead * behind > 0, jnp.where(ahead > 0, smaller, -smaller), jnp.zeros_like(smaller)
    )


def face_flux(before, center, after, beyond, vel_here, vel_next, wet_here, wet_next):
    courant = 0.5 * (vel_here + vel_next) * wet_here * wet_next
    upwind_pos = center + 0.5 * (1.0 - courant) * limited_slope(after - center, center - before)
    upwind_neg = after - 0.5 * (1.0 + courant) * limited_slope(beyond - after, after - center)
    return courant * jnp.where(courant >= 0, upwind_pos, upwind_neg)


def transport(field, flow_east, flow_north, wet):
    free_top_height, width = (field.shape[-2], field.shape[-1])
    rows = slice(2, free_top_height - 2)
    cols = slice(2, width - 2)
    flux_x = face_flux(
        field[..., rows, 0 : width - 3],
        field[..., rows, 1 : width - 2],
        field[..., rows, 2 : width - 1],
        field[..., rows, 3:width],
        flow_east[..., rows, 1 : width - 2],
        flow_east[..., rows, 2 : width - 1],
        wet[..., rows, 1 : width - 2],
        wet[..., rows, 2 : width - 1],
    )
    flux_y = face_flux(
        field[..., 0 : free_top_height - 3, cols],
        field[..., 1 : free_top_height - 2, cols],
        field[..., 2 : free_top_height - 1, cols],
        field[..., 3:free_top_height, cols],
        flow_north[..., 1 : free_top_height - 2, cols],
        flow_north[..., 2 : free_top_height - 1, cols],
        wet[..., 1 : free_top_height - 2, cols],
        wet[..., 2 : free_top_height - 1, cols],
    )
    return (
        field[..., rows, cols]
        - (flux_x[..., 1:] - flux_x[..., :-1])
        - (flux_y[..., 1:, :] - flux_y[..., :-1, :])
    )


def ocean_core(stacked, north, south, east, west, wet, coriolis):
    count = (stacked.shape[0] - 1) // 2
    zonal_flow_value = stacked[:count]
    meridional_flow_value = stacked[count : 2 * count]
    free_top_height = stacked[2 * count]
    lap_east = north[:count] + south[:count] + east[:count] + west[:count] - 4.0 * zonal_flow_value
    lap_north = (
        north[count : 2 * count]
        + south[count : 2 * count]
        + east[count : 2 * count]
        + west[count : 2 * count]
        - 4.0 * meridional_flow_value
    )
    grad_x = 0.5 * (east[2 * count] - west[2 * count])
    grad_y = 0.5 * (north[2 * count] - south[2 * count])
    div_levels = 0.5 * (east[:count] - west[:count]) + 0.5 * (
        north[count : 2 * count] - south[count : 2 * count]
    )
    new_east = wet * (
        zonal_flow_value
        + TIME_STEP
        * (
            coriolis * meridional_flow_value
            - GRAVITY * grad_x
            + VISCOSITY * lap_east
            - BOTTOM_DRAG * zonal_flow_value
        )
    )
    new_north = wet * (
        meridional_flow_value
        + TIME_STEP
        * (
            -coriolis * zonal_flow_value
            - GRAVITY * grad_y
            + VISCOSITY * lap_north
            - BOTTOM_DRAG * meridional_flow_value
        )
    )
    return (new_east, new_north, free_top_height, jnp.sum(div_levels, 0))


def ocean_step(zonal_flow_value, meridional_flow_value, free_top_height, wet, coriolis):
    stacked = jnp.concatenate([zonal_flow_value, meridional_flow_value, free_top_height[None]], 0)
    by_lat = padded(stacked, (("lat", 1),), 1, False)
    by_lon = padded(stacked, (("lon", 2),), 1, True)
    new_east, new_north, free_top_height, partial_div = ocean_core(
        stacked,
        by_lat[:, 2:, :],
        by_lat[:, :-2, :],
        by_lon[:, :, 2:],
        by_lon[:, :, :-2],
        wet,
        coriolis,
    )
    divergence = lax.psum(partial_div, "trc")
    return (new_east, new_north, free_top_height - TIME_STEP * DEPTH_SCALE * divergence)


def widen_flow(flow, width):
    rows_ext = padded(flow, (("lat", 2),), width, False)
    return padded(rows_ext, (("lon", 3),), width, True)


def widen_tracers(field, width):
    rows_ext = padded(field, (("lat", 2),), width, False)
    return padded(rows_ext, (("lon", 3),), width, True)


def light_profile(absorbed, wet, surface):
    levels = absorbed.shape[0]
    layer = COLUMN_DEPTH / levels * (WATER_ABSORB + absorbed) * wet
    above = jnp.cumsum(layer, 0) - layer
    top_light = surface[None, :, None] * jnp.exp(-above)
    return (top_light * (1.0 - jnp.exp(-layer)), top_light / (top_light + HALF_LIGHT))


def body(
    species_concentrations,
    zonal_velocity_array,
    meridional_velocity_array,
    thermal_anomaly,
    ocean_top_height_grid,
    water_layer_tally,
    species_interaction_table,
    species_production_pace,
    photon_uptake,
):
    tracer_count, levels, lat_rows, lon_cols = species_concentrations.shape
    own_levels = zonal_velocity_array.shape[0]
    trc_place = lax.axis_index("trc")
    lat_total = lat_rows * lax.axis_size("lat")
    lat_global = (lax.axis_index("lat") * lat_rows + jnp.arange(lat_rows)).astype(jnp.float32)
    angle = math.pi * ((lat_global + 0.5) / lat_total - 0.5)
    coriolis = CORIOLIS_SCALE * jnp.sin(angle)[:, None]
    surface = 1.0 + jnp.cos(angle)
    depth_index = jnp.arange(levels)
    wet_all = (depth_index[:, None, None] < water_layer_tally[None]).astype(jnp.float32)
    wet_own = lax.dynamic_slice_in_dim(wet_all, trc_place * own_levels, own_levels, 0)
    east_start = wet_own * zonal_velocity_array
    north_start = wet_own * meridional_velocity_array
    zonal_flow_value, meridional_flow_value, free_top_height = (
        east_start,
        north_start,
        ocean_top_height_grid,
    )
    for substep in range(2):
        zonal_flow_value, meridional_flow_value, free_top_height = ocean_step(
            zonal_flow_value, meridional_flow_value, free_top_height, wet_own, coriolis
        )
    velocity = lax.all_gather(jnp.stack([east_start, north_start]), "trc", axis=1, tiled=True)
    flow = jnp.concatenate([velocity, wet_all[None]], 0)
    flow_ext = widen_flow(flow, 4)
    first = transport(
        widen_tracers(species_concentrations, 4), flow_ext[0], flow_ext[1], flow_ext[2]
    )
    inner = flow_ext[:, :, 2:-2, 2:-2]
    moved = transport(first, inner[0], inner[1], inner[2])
    share = lat_rows // lax.axis_size("trc")
    columns = lax.all_to_all(moved, "trc", split_axis=2, concat_axis=0, tiled=True)
    wet_cols = lax.dynamic_slice_in_dim(wet_all, trc_place * share, share, 1)
    surface_cols = lax.dynamic_slice_in_dim(surface, trc_place * share, share, 0)
    absorbed = jnp.einsum("n,nkyx->kyx", photon_uptake, jnp.abs(columns), precision=HIGHEST)
    solar_warming, light_factor = light_profile(absorbed, wet_cols, surface_cols)
    mixed = jnp.einsum("mn,nkyx->mkyx", species_interaction_table, columns, precision=HIGHEST)
    species_postchemistry = columns + wet_cols * REACT_STEP * (
        mixed + species_production_pace[:, None, None, None] * light_factor * columns
    )
    updated_tracers = lax.all_to_all(
        species_postchemistry, "trc", split_axis=0, concat_axis=2, tiled=True
    )
    pointwise_warming_pace = lax.all_to_all(
        solar_warming, "trc", split_axis=0, concat_axis=1, tiled=True
    )
    return (
        updated_tracers,
        zonal_flow_value,
        meridional_flow_value,
        thermal_anomaly + WARMING_WEIGHT * pointwise_warming_pace,
        free_top_height,
    )


def solution(mesh):
    return jax.shard_map(
        body,
        mesh=mesh,
        in_specs=(
            P("trc", None, "lat", "lon"),
            P("trc", "lat", "lon"),
            P("trc", "lat", "lon"),
            P("trc", "lat", "lon"),
            P("lat", "lon"),
            P("lat", "lon"),
            P(),
            P(),
            P(),
        ),
        out_specs=(
            P("trc", None, "lat", "lon"),
            P("trc", "lat", "lon"),
            P("trc", "lat", "lon"),
            P("trc", "lat", "lon"),
            P("lat", "lon"),
        ),
        check_vma=False,
    )
```

profile of v0, /device:TPU:0, one launch (start us, length us, event | category | flops | bytes accessed | tf_op | source)
XLA Modules:
  0.0 207.8 jit_solution(16878511505992361957)
XLA Ops:
  3.0 15.7 %all_gather.3 = f32[2,8,32,128]{3,2,0,1:T(8,128)S(1)} all-gather(f32[2,2,32,128]{3,2,0,1:T(8,128)S(1)} %pad_maximum_fusion.8), channel_id=1, replica_groups=mesh['trc'=4,'lat'=4,'lon'=2] {'trc'}, dimensions={1}, use_global_device_ids=true | all-gather | bytes 327680 | tf_op jit(solution)/shard_map/all_gather | solution.py:190
  20.2 3.0 %collective-permute-start.4 = (f32[3,8,4,128]{3,1,2,0:T(8,128)S(1)}, f32[3,8,4,128]{3,1,2,0:T(8,128)S(1)}, u32[]{:S(2)}, u32[]{:S(2)}) collective-permute-start(f32[3,8,4,128]{3,1,2,0:T(8,128)S(1)} %get-tuple-element.30), channel_id=1, source_target_pairs={{0,2},{2,4},{4,6},{1,3},{3,5},{5,7},{8,10},{10,12},{12,14},{9,11},... | collective-permute-start | bytes 147464 | tf_op jit(solution)/shard_map/ppermute | solution.py:28
  29.7 4.0 %collective-permute-start = (f32[8,8,4,128]{3,1,2,0:T(8,128)}, f32[8,8,4,128]{3,1,2,0:T(8,128)}, u32[]{:S(2)}, u32[]{:S(2)}) collective-permute-start(f32[8,8,4,128]{3,1,2,0:T(8,128)} %copy.159), channel_id=1, source_target_pairs={{0,2},{2,4},{4,6},{1,3},{3,5},{5,7},{8,10},{10,12},{12,14},{9,11},... | collective-permute-start | bytes 393224 | tf_op jit(solution)/shard_map/ppermute | solution.py:28
  33.7 2.7 %copy.131 = f32[8,8,32,128]{2,1,3,0:T(8,128)} copy(f32[8,8,32,128]{3,2,1,0:T(8,128)S(1)} %copy-done.8) | data formatting | bytes 2097152 | tf_op args[0]
  36.4 2.5 %collective-permute-done.7 = f32[3,8,40,4]{3,1,2,0:T(8,128)S(1)} collective-permute-done((f32[3,8,40,4]{3,1,2,0:T(8,128)}, f32[3,8,40,4]{3,1,2,0:T(8,128)S(1)}, u32[]{:S(2)}, u32[]{:S(2)}) %collective-permute-start.7) | collective-permute-done | bytes 15392 | tf_op jit(solution)/shard_map/ppermute | solution.py:31
  38.9 10.5 %collective-permute-done.6 = f32[3,8,40,4]{3,1,2,0:T(8,128)S(1)} collective-permute-done((f32[3,8,40,4]{3,1,2,0:T(8,128)S(1)}, f32[3,8,40,4]{3,1,2,0:T(8,128)S(1)}, u32[]{:S(2)}, u32[]{:S(2)}) %collective-permute-start.6) | collective-permute-done | bytes 15392 | tf_op jit(solution)/shard_map/ppermute | solution.py:28
  55.2 3.6 %copy.132 = f32[8,8,4,128]{2,1,3,0:T(8,128)} copy(f32[8,8,4,128]{3,1,2,0:T(8,128)} %collective-permute-done.1) | data formatting | bytes 262144 | tf_op jit(solution)/shard_map/ppermute | solution.py:31
  58.8 3.5 %copy.130 = f32[8,8,4,128]{2,1,3,0:T(8,128)} copy(f32[8,8,4,128]{3,1,2,0:T(8,128)} %collective-permute-done) | data formatting | bytes 262144 | tf_op jit(solution)/shard_map/ppermute | solution.py:28
  62.3 2.1 %pad_maximum_fusion.5 = (f32[8,8,40,4]{2,1,3,0:T(8,128)}, f32[8,8,40,4]{2,1,3,0:T(8,128)}) fusion(f32[8,8,4,128]{2,1,3,0:T(8,128)} %copy.132, f32[8,8,32,128]{2,1,3,0:T(8,128)} %copy.131, f32[8,8,4,128]{2,1,3,0:T(8,128)} %copy.130), kind=kLoop, calls=%fused_computation.120 | loop fusion | flops 40960 | bytes 1392640 | tf_op jit(solution)/shard_map/slice | solution.py:29
  76.3 1.9 copy.150
  80.4 2.1 %copy.146 = f32[8,32,129]{1,0,2:T(8,128)} copy(f32[8,32,129]{2,0,1:T(8,128)} %get-tuple-element.37) | data formatting | bytes 264192 | tf_op jit(solution)/shard_map/mul | solution.py:46
  82.5 2.1 %copy.145 = f32[8,32,129]{1,0,2:T(8,128)} copy(f32[8,32,129]{2,0,1:T(8,128)} %get-tuple-element.36) | data formatting | bytes 264192 | tf_op jit(solution)/shard_map/mul | solution.py:45
  85.9 6.0 %pad_maximum_fusion = f32[8,8,40,136]{2,1,3,0:T(8,128)S(1)} fusion(f32[8,8,40,4]{2,1,3,0:T(8,128)} %collective-permute-done.3, f32[8,8,4,128]{2,1,3,0:T(8,128)} %copy.132, f32[8,8,32,128]{2,1,3,0:T(8,128)} %copy.131, f32[8,8,4,128]{2,1,3,0:T(8,128)} %copy.130, f32[8,8,40,4]{2,1,3,0:T(8,128)} %collective-permute-done.2), kind=kLoop, calls=%fused_computation.8 | loop fusion | flops 1392640 | bytes 2785280 | tf_op jit(solution)/shard_map/concatenate | solution.py:32
  91.8 4.3 %fusion.12 = f32[8,8,37,132]{2,1,3,0:T(8,128)S(1)} fusion(f32[8,8,40,136]{2,1,3,0:T(8,128)S(1)} %pad_maximum_fusion, f32[8,37,132]{1,0,2:T(8,128)S(1)} %copy.142, f32[8,37,132]{1,0,2:T(8,128)S(1)} %copy-done.1, f32[8,37,132]{1,0,2:T(8,128)S(1)} %copy.139, pred[8,37,132]{1,0,2:T(8,128)(4,1)S(1)} %copy.140), kind=kLoop, calls=%fused_computation.26 | loop fusion | flops 8126976 | bytes 6759456 | tf_op jit(solution)/shard_map/mul | solution.py:47
  96.1 5.1 %fusion.4 = f32[8,8,36,133]{2,1,3,0:T(8,128)S(1)} fusion(f32[8,8,40,136]{2,1,3,0:T(8,128)S(1)} %pad_maximum_fusion, f32[8,36,133]{1,0,2:T(8,128)S(1)} %copy.138, f32[8,36,133]{1,0,2:T(8,128)S(1)} %copy.137, f32[8,36,133]{1,0,2:T(8,128)S(1)} %copy.135, pred[8,36,133]{1,0,2:T(8,128)(4,1)S(1)} %copy.136), kind=kLoop, calls=%fused_computation.13 | loop fusion | flops 7967232 | bytes 6626592 | tf_op jit(solution)/shard_map/mul | solution.py:47
  101.3 2.6 %fusion.16 = f32[8,8,36,132]{2,1,3,0:T(8,128)S(1)} fusion(f32[8,8,37,132]{2,1,3,0:T(8,128)S(1)} %fusion.12, f32[8,8,36,133]{2,1,3,0:T(8,128)S(1)} %fusion.4, f32[8,8,40,136]{2,1,3,0:T(8,128)S(1)} %pad_maximum_fusion), kind=kLoop, calls=%fused_computation.31 | loop fusion | flops 1216512 | bytes 7299072 | tf_op jit(solution)/shard_map/sub | solution.py:75
  103.9 4.2 %fusion.30 = f32[8,8,33,128]{2,1,3,0:T(8,128)S(1)} fusion(f32[8,8,36,132]{2,1,3,0:T(8,128)S(1)} %fusion.16, f32[8,33,128]{1,0,2:T(8,128)S(1)} %copy-done.6, f32[8,33,128]{1,0,2:T(8,128)S(1)} %copy-done.7, f32[8,33,128]{1,0,2:T(8,128)S(1)} %copy-done.5, pred[8,33,128]{1,0,2:T(8,128)(4,1)S(1)} %copy.148), kind=kLoop, calls=%fused_computation.56 | loop fusion | flops 7028736 | bytes 5846016 | tf_op jit(solution)/shard_map/mul | solution.py:47
  108.1 4.7 %fusion.22 = f32[8,8,32,129]{2,1,3,0:T(8,128)S(1)} fusion(f32[8,8,36,132]{2,1,3,0:T(8,128)S(1)} %fusion.16, f32[8,32,129]{1,0,2:T(8,128)S(1)} %copy-done.3, f32[8,32,129]{1,0,2:T(8,128)S(1)} %copy-done.4, f32[8,32,129]{1,0,2:T(8,128)S(1)} %copy-done.2, pred[8,32,129]{1,0,2:T(8,128)(4,1)S(1)} %copy.144), kind=kLoop, calls=%fused_computation.43 | loop fusion | flops 6868992 | bytes 5713152 | tf_op jit(solution)/shard_map/mul | solution.py:47
  112.9 3.8 %fusion.34 = f32[8,8,32,128]{2,1,3,0:T(8,128)} fusion(f32[8,8,33,128]{2,1,3,0:T(8,128)S(1)} %fusion.30, f32[8,8,32,129]{2,1,3,0:T(8,128)S(1)} %fusion.22, f32[8,8,36,132]{2,1,3,0:T(8,128)S(1)} %fusion.16), kind=kLoop, calls=%fused_computation.61 | loop fusion | flops 1048576 | bytes 6291456 | tf_op jit(solution)/shard_map/sub | solution.py:75
  116.6 3.9 %copy.151 = f32[8,8,32,128]{3,1,0,2:T(8,128)} copy(f32[8,8,32,128]{2,1,3,0:T(8,128)} %fusion.34) | data formatting | bytes 2097152 | tf_op jit(solution)/shard_map/sub | solution.py:75
  120.6 5.2 %all-to-all-start = ((f32[8,8,32,128]{3,1,0,2:T(8,128)}), f32[8,8,32,128]{3,1,0,2:T(8,128)S(1)}, u32[]{:S(2)}, u32[]{:S(2)}) async-start(f32[8,8,32,128]{3,1,0,2:T(8,128)} %copy.151), calls=%async_computation | async-start | bytes 2097152 | tf_op jit(solution)/shard_map/all_to_all | solution.py:199
  128.5 1.6 collective-permute-start.9
  130.8 2.2 %collective-permute-done.9 = f32[5,32,1]{2,1,0:T(8,128)S(1)} collective-permute-done((f32[5,32,1]{2,1,0:T(8,128)S(1)}, f32[5,32,1]{2,1,0:T(8,128)S(1)}, u32[]{:S(2)}, u32[]{:S(2)}) %collective-permute-start.9) | collective-permute-done | bytes 672 | tf_op jit(solution)/shard_map/ppermute | solution.py:28
  133.0 2.2 %collective-permute-done.8 = f32[5,32,1]{2,1,0:T(8,128)S(1)} collective-permute-done((f32[5,32,1]{2,1,0:T(8,128)S(1)}, f32[5,32,1]{2,1,0:T(8,128)S(1)}, u32[]{:S(2)}, u32[]{:S(2)}) %collective-permute-start.8) | collective-permute-done | bytes 672 | tf_op jit(solution)/shard_map/ppermute | solution.py:31
  135.4 24.5 %psum.14 = f32[32,128]{1,0:T(8,128)S(1)} all-reduce(f32[32,128]{1,0:T(8,128)S(1)} %multiply_reduce_fusion.1), channel_id=1, replica_groups=mesh['trc'=4,'lat'=4,'lon'=2] {'trc'}, use_global_device_ids=true, to_apply=%region_2.0 | all-reduce | flops 4096 | bytes 32768 | tf_op jit(solution)/shard_map/psum | solution.py:135
  161.7 3.4 %all-to-all-start.2 = ((f32[8,8,128]{2,1,0:T(8,128)}), f32[8,8,128]{2,1,0:T(8,128)S(1)}, u32[]{:S(2)}, u32[]{:S(2)}) async-start(f32[8,8,128]{2,1,0:T(8,128)} %get-tuple-element.40), calls=%async_computation.2 | async-start | bytes 65536 | tf_op jit(solution)/shard_map/all_to_all | solution.py:211
  168.0 2.7 %all-to-all-done.2 = f32[8,8,128]{2,1,0:T(8,128)S(1)} async-done(((f32[8,8,128]{2,1,0:T(8,128)}), f32[8,8,128]{2,1,0:T(8,128)S(1)}, u32[]{:S(2)}, u32[]{:S(2)}) %all-to-all-start.2) | async-done | bytes 32800 | tf_op jit(solution)/shard_map/all_to_all | solution.py:211
  170.7 3.5 %all-to-all-start.1 = ((f32[32,8,8,128]{3,2,1,0:T(8,128)}), f32[32,8,8,128]{3,2,1,0:T(8,128)S(1)}, u32[]{:S(2)}, u32[]{:S(2)}) async-start(f32[32,8,8,128]{3,2,1,0:T(8,128)} %copy.153), calls=%async_computation.1 | async-start | bytes 2097152 | tf_op jit(solution)/shard_map/all_to_all | solution.py:208
  177.0 1.6 collective-permute-start.13
  179.1 3.1 %collective-permute-done.13 = f32[5,32,1]{2,1,0:T(8,128)S(1)} collective-permute-done((f32[5,32,1]{2,1,0:T(8,128)S(1)}, f32[5,32,1]{2,1,0:T(8,128)S(1)}, u32[]{:S(2)}, u32[]{:S(2)}) %collective-permute-start.13) | collective-permute-done | bytes 672 | tf_op jit(solution)/shard_map/ppermute | solution.py:28
  182.2 1.8 collective-permute-done.12
  184.1 19.9 %psum.15 = f32[32,128]{1,0:T(8,128)S(1)} all-reduce(f32[32,128]{1,0:T(8,128)S(1)} %multiply_reduce_fusion), channel_id=1, replica_groups=mesh['trc'=4,'lat'=4,'lon'=2] {'trc'}, use_global_device_ids=true, to_apply=%region_4.5 | all-reduce | flops 4096 | bytes 32768 | tf_op jit(solution)/shard_map/psum | solution.py:135
  (112 shorter events, 46.6 us)
Async XLA Ops:
  0.6 164.5 %copy-start = (f32[32,32]{1,0:T(8,128)S(1)}, f32[32,32]{1,0:T(8,128)}, u32[]{:S(2)}) copy-start(f32[32,32]{1,0:T(8,128)} %param.15) | copy-start | bytes 12292
  0.6 26.4 %copy-start.8 = (f32[8,8,32,128]{3,2,1,0:T(8,128)S(1)}, f32[8,8,32,128]{3,2,1,0:T(8,128)}, u32[]{:S(2)}) copy-start(f32[8,8,32,128]{3,2,1,0:T(8,128)} %param.9) | copy-start | bytes 3145732
  18.9 4.3 %collective-permute-start.5 = (f32[3,8,4,128]{3,1,2,0:T(8,128)S(1)}, f32[3,8,4,128]{3,1,2,0:T(8,128)S(1)}, u32[]{:S(2)}, u32[]{:S(2)}) collective-permute-start(f32[3,8,4,128]{3,1,2,0:T(8,128)S(1)} %get-tuple-element.31), channel_id=1, source_target_pairs={{2,0},{4,2},{6,4},{3,1},{5,3},{7,5},{10,8},{12,10},{14,12},{11,9},... | collective-permute-start | bytes 147464 | tf_op jit(solution)/shard_map/ppermute | solution.py:31
  20.2 3.9 %collective-permute-start.4 = (f32[3,8,4,128]{3,1,2,0:T(8,128)S(1)}, f32[3,8,4,128]{3,1,2,0:T(8,128)S(1)}, u32[]{:S(2)}, u32[]{:S(2)}) collective-permute-start(f32[3,8,4,128]{3,1,2,0:T(8,128)S(1)} %get-tuple-element.30), channel_id=1, source_target_pairs={{0,2},{2,4},{4,6},{1,3},{3,5},{5,7},{8,10},{10,12},{12,14},{9,11},... | collective-permute-start | bytes 147464 | tf_op jit(solution)/shard_map/ppermute | solution.py:28
  25.0 13.9 %collective-permute-start.7 = (f32[3,8,40,4]{3,1,2,0:T(8,128)}, f32[3,8,40,4]{3,1,2,0:T(8,128)S(1)}, u32[]{:S(2)}, u32[]{:S(2)}) collective-permute-start(f32[3,8,40,4]{3,1,2,0:T(8,128)} %get-tuple-element.29), channel_id=1, source_target_pairs={{1,0},{0,1},{3,2},{2,3},{5,4},{4,5},{7,6},{6,7},{9,8},{8,9},{11,10... | collective-permute-start | bytes 46088 | tf_op jit(solution)/shard_map/ppermute | solution.py:31
  26.5 22.9 %collective-permute-start.6 = (f32[3,8,40,4]{3,1,2,0:T(8,128)S(1)}, f32[3,8,40,4]{3,1,2,0:T(8,128)S(1)}, u32[]{:S(2)}, u32[]{:S(2)}) collective-permute-start(f32[3,8,40,4]{3,1,2,0:T(8,128)S(1)} %get-tuple-element.28), channel_id=1, source_target_pairs={{0,1},{1,0},{2,3},{3,2},{4,5},{5,4},{6,7},{7,6},{8,9},{9,8},{10,11... | collective-permute-start | bytes 46088 | tf_op jit(solution)/shard_map/ppermute | solution.py:28
  27.8 27.4 %collective-permute-start.1 = (f32[8,8,4,128]{3,1,2,0:T(8,128)}, f32[8,8,4,128]{3,1,2,0:T(8,128)}, u32[]{:S(2)}, u32[]{:S(2)}) collective-permute-start(f32[8,8,4,128]{3,1,2,0:T(8,128)} %copy.160), channel_id=1, source_target_pairs={{2,0},{4,2},{6,4},{3,1},{5,3},{7,5},{10,8},{12,10},{14,12},{11,9},... | collective-permute-start | bytes 393224 | tf_op jit(solution)/shard_map/ppermute | solution.py:31
  29.7 29.1 %collective-permute-start = (f32[8,8,4,128]{3,1,2,0:T(8,128)}, f32[8,8,4,128]{3,1,2,0:T(8,128)}, u32[]{:S(2)}, u32[]{:S(2)}) collective-permute-start(f32[8,8,4,128]{3,1,2,0:T(8,128)} %copy.159), channel_id=1, source_target_pairs={{0,2},{2,4},{4,6},{1,3},{3,5},{5,7},{8,10},{10,12},{12,14},{9,11},... | collective-permute-start | bytes 393224 | tf_op jit(solution)/shard_map/ppermute | solution.py:28
  64.4 21.4 %collective-permute-start.3 = (f32[8,8,40,4]{2,1,3,0:T(8,128)}, f32[8,8,40,4]{2,1,3,0:T(8,128)}, u32[]{:S(2)}, u32[]{:S(2)}) collective-permute-start(f32[8,8,40,4]{2,1,3,0:T(8,128)} %get-tuple-element.19), channel_id=1, source_target_pairs={{1,0},{0,1},{3,2},{2,3},{5,4},{4,5},{7,6},{6,7},{9,8},{8,9},{11,10... | collective-permute-start | bytes 122888 | tf_op jit(solution)/shard_map/ppermute | solution.py:31
  65.9 19.9 %collective-permute-start.2 = (f32[8,8,40,4]{2,1,3,0:T(8,128)}, f32[8,8,40,4]{2,1,3,0:T(8,128)}, u32[]{:S(2)}, u32[]{:S(2)}) collective-permute-start(f32[8,8,40,4]{2,1,3,0:T(8,128)} %get-tuple-element.18), channel_id=1, source_target_pairs={{0,1},{1,0},{2,3},{3,2},{4,5},{5,4},{6,7},{7,6},{8,9},{9,8},{10,11... | collective-permute-start | bytes 122888 | tf_op jit(solution)/shard_map/ppermute | solution.py:28
  70.2 8.0 %copy-start.10 = (f32[8,33,128]{2,0,1:T(8,128)S(1)}, f32[8,33,128]{2,0,1:T(8,128)}, u32[]{:S(2)}) copy-start(f32[8,33,128]{2,0,1:T(8,128)} %get-tuple-element.38) | copy-start | bytes 405508
  85.8 6.0 %copy-start.1 = (f32[8,37,132]{1,0,2:T(8,128)S(1)}, f32[8,37,132]{1,0,2:T(8,128)}, u32[]{:S(2)}) copy-start(f32[8,37,132]{1,0,2:T(8,128)} %copy.141) | copy-start | bytes 468868
  101.2 2.6 %copy-start.5 = (f32[8,33,128]{1,0,2:T(8,128)S(1)}, f32[8,33,128]{1,0,2:T(8,128)}, u32[]{:S(2)}) copy-start(f32[8,33,128]{1,0,2:T(8,128)} %copy.147) | copy-start | bytes 405508
  101.3 2.6 %copy-start.6 = (f32[8,33,128]{1,0,2:T(8,128)S(1)}, f32[8,33,128]{1,0,2:T(8,128)}, u32[]{:S(2)}) copy-start(f32[8,33,128]{1,0,2:T(8,128)} %copy.150) | copy-start | bytes 405508
  103.9 4.3 %copy-start.2 = (f32[8,32,129]{1,0,2:T(8,128)S(1)}, f32[8,32,129]{1,0,2:T(8,128)}, u32[]{:S(2)}) copy-start(f32[8,32,129]{1,0,2:T(8,128)} %copy.143) | copy-start | bytes 396292
  103.9 4.3 %copy-start.3 = (f32[8,32,129]{1,0,2:T(8,128)S(1)}, f32[8,32,129]{1,0,2:T(8,128)}, u32[]{:S(2)}) copy-start(f32[8,32,129]{1,0,2:T(8,128)} %copy.146) | copy-start | bytes 396292
  103.9 4.3 %copy-start.4 = (f32[8,32,129]{1,0,2:T(8,128)S(1)}, f32[8,32,129]{1,0,2:T(8,128)}, u32[]{:S(2)}) copy-start(f32[8,32,129]{1,0,2:T(8,128)} %copy.145) | copy-start | bytes 396292
  116.6 9.1 %copy-start.9 = (f32[32,128]{1,0:T(8,128)S(1)}, f32[32,128]{1,0:T(8,128)}, u32[]{:S(2)}) copy-start(f32[32,128]{1,0:T(8,128)} %param.13) | copy-start | bytes 49156
  116.6 43.5 %copy-start.12 = (f32[32]{0:T(128)S(1)}, f32[32]{0:T(128)}, u32[]{:S(2)}) copy-start(f32[32]{0:T(128)} %param.17) | copy-start | bytes 388
  116.6 48.5 %copy-start.13 = (f32[32]{0:T(128)S(1)}, f32[32]{0:T(128)}, u32[]{:S(2)}) copy-start(f32[32]{0:T(128)} %param.16) | copy-start | bytes 388
  120.6 39.6 %all-to-all-start = ((f32[8,8,32,128]{3,1,0,2:T(8,128)}), f32[8,8,32,128]{3,1,0,2:T(8,128)S(1)}, u32[]{:S(2)}, u32[]{:S(2)}) async-start(f32[8,8,32,128]{3,1,0,2:T(8,128)} %copy.151), calls=%async_computation | async-start | bytes 2097152 | tf_op jit(solution)/shard_map/all_to_all | solution.py:199
  125.8 9.5 %collective-permute-start.11 = (f32[5,1,128]{2,1,0:T(1,128)S(1)}, f32[5,1,128]{2,1,0:T(1,128)S(1)}, u32[]{:S(2)}, u32[]{:S(2)}) collective-permute-start(f32[5,1,128]{2,1,0:T(1,128)S(1)} %get-tuple-element.55), channel_id=1, source_target_pairs={{0,2},{2,4},{4,6},{1,3},{3,5},{5,7},{8,10},{10,12},{12,14},{9,11},... | collective-permute-start | bytes 7688 | tf_op jit(solution)/shard_map/ppermute | solution.py:28
  127.1 8.2 %collective-permute-start.10 = (f32[5,1,128]{2,1,0:T(1,128)S(1)}, f32[5,1,128]{2,1,0:T(1,128)S(1)}, u32[]{:S(2)}, u32[]{:S(2)}) collective-permute-start(f32[5,1,128]{2,1,0:T(1,128)S(1)} %get-tuple-element.54), channel_id=1, source_target_pairs={{2,0},{4,2},{6,4},{3,1},{5,3},{7,5},{10,8},{12,10},{14,12},{11,9},... | collective-permute-start | bytes 7688 | tf_op jit(solution)/shard_map/ppermute | solution.py:31
  128.5 4.5 %collective-permute-start.9 = (f32[5,32,1]{2,1,0:T(8,128)S(1)}, f32[5,32,1]{2,1,0:T(8,128)S(1)}, u32[]{:S(2)}, u32[]{:S(2)}) collective-permute-start(f32[5,32,1]{2,1,0:T(8,128)S(1)} %get-tuple-element.53), channel_id=1, source_target_pairs={{0,1},{1,0},{2,3},{3,2},{4,5},{5,4},{6,7},{7,6},{8,9},{9,8},{10,11... | collective-permute-start | bytes 1928 | tf_op jit(solution)/shard_map/ppermute | solution.py:28
  130.1 5.2 %collective-permute-start.8 = (f32[5,32,1]{2,1,0:T(8,128)S(1)}, f32[5,32,1]{2,1,0:T(8,128)S(1)}, u32[]{:S(2)}, u32[]{:S(2)}) collective-permute-start(f32[5,32,1]{2,1,0:T(8,128)S(1)} %get-tuple-element.52), channel_id=1, source_target_pairs={{1,0},{0,1},{3,2},{2,3},{5,4},{4,5},{7,6},{6,7},{9,8},{8,9},{11,10... | collective-permute-start | bytes 1928 | tf_op jit(solution)/shard_map/ppermute | solution.py:31
  161.7 44.4 %copy-start.11 = (f32[2,32,128]{2,1,0:T(8,128)S(1)}, f32[2,32,128]{2,1,0:T(8,128)}, u32[]{:S(2)}) copy-start(f32[2,32,128]{2,1,0:T(8,128)} %param.12) | copy-start | bytes 98308
  161.7 9.0 %all-to-all-start.2 = ((f32[8,8,128]{2,1,0:T(8,128)}), f32[8,8,128]{2,1,0:T(8,128)S(1)}, u32[]{:S(2)}, u32[]{:S(2)}) async-start(f32[8,8,128]{2,1,0:T(8,128)} %get-tuple-element.40), calls=%async_computation.2 | async-start | bytes 65536 | tf_op jit(solution)/shard_map/all_to_all | solution.py:211
  170.7 36.0 %all-to-all-start.1 = ((f32[32,8,8,128]{3,2,1,0:T(8,128)}), f32[32,8,8,128]{3,2,1,0:T(8,128)S(1)}, u32[]{:S(2)}, u32[]{:S(2)}) async-start(f32[32,8,8,128]{3,2,1,0:T(8,128)} %copy.153), calls=%async_computation.1 | async-start | bytes 2097152 | tf_op jit(solution)/shard_map/all_to_all | solution.py:208
  174.3 9.7 %collective-permute-start.15 = (f32[5,1,128]{2,1,0:T(1,128)S(1)}, f32[5,1,128]{2,1,0:T(1,128)S(1)}, u32[]{:S(2)}, u32[]{:S(2)}) collective-permute-start(f32[5,1,128]{2,1,0:T(1,128)S(1)} %get-tuple-element.49), channel_id=1, source_target_pairs={{0,2},{2,4},{4,6},{1,3},{3,5},{5,7},{8,10},{10,12},{12,14},{9,11},... | collective-permute-start | bytes 7688 | tf_op jit(solution)/shard_map/ppermute | solution.py:28
  175.6 8.4 %collective-permute-start.14 = (f32[5,1,128]{2,1,0:T(1,128)S(1)}, f32[5,1,128]{2,1,0:T(1,128)S(1)}, u32[]{:S(2)}, u32[]{:S(2)}) collective-permute-start(f32[5,1,128]{2,1,0:T(1,128)S(1)} %get-tuple-element.48), channel_id=1, source_target_pairs={{2,0},{4,2},{6,4},{3,1},{5,3},{7,5},{10,8},{12,10},{14,12},{11,9},... | collective-permute-start | bytes 7688 | tf_op jit(solution)/shard_map/ppermute | solution.py:31
  177.0 5.2 %collective-permute-start.13 = (f32[5,32,1]{2,1,0:T(8,128)S(1)}, f32[5,32,1]{2,1,0:T(8,128)S(1)}, u32[]{:S(2)}, u32[]{:S(2)}) collective-permute-start(f32[5,32,1]{2,1,0:T(8,128)S(1)} %get-tuple-element.47), channel_id=1, source_target_pairs={{0,1},{1,0},{2,3},{3,2},{4,5},{5,4},{6,7},{7,6},{8,9},{9,8},{10,11... | collective-permute-start | bytes 1928 | tf_op jit(solution)/shard_map/ppermute | solution.py:28
  178.6 5.4 %collective-permute-start.12 = (f32[5,32,1]{2,1,0:T(8,128)S(1)}, f32[5,32,1]{2,1,0:T(8,128)S(1)}, u32[]{:S(2)}, u32[]{:S(2)}) collective-permute-start(f32[5,32,1]{2,1,0:T(8,128)S(1)} %get-tuple-element.46), channel_id=1, source_target_pairs={{1,0},{0,1},{3,2},{2,3},{5,4},{4,5},{7,6},{6,7},{9,8},{8,9},{11,10... | collective-permute-start | bytes 1928 | tf_op jit(solution)/shard_map/ppermute | solution.py:31
  (1 other events, 2.6 us)
where the time goes:
time: 209 us; the launch traced here: 208 us
  blocking collectives  60 us (29%)
  other arithmetic  45.3 us (22%)
  local copies, waits for them, and re-layouts  38.1 us (18%)
  starting transfers between devices  35.1 us (17%)
  waiting for transfers between devices  26 us (12%)
  matrix products  2.11 us (1%)
    psum x2, blocking collectives, ocean_step(): divergence = lax.psum(partial_div, 'trc')  44.3 us
    mul x4, other arithmetic, face_flux(): return courant * jnp.where(courant >= 0, upwind_pos, upwind_neg)  18.3 us
    ppermute x8, waiting for transfers between devices, padded(): lax.ppermute(lax.slice_in_dim(block, block.shape[dim] - width, None, axis...  16.8 us
    all_gather x1, blocking collectives, body(): lax.all_gather(jnp.stack([east_start, north_start]), 'trc', axis=1, tiled...  15.7 us
    ppermute x8, starting transfers between devices, padded(): lax.ppermute(lax.slice_in_dim(block, block.shape[dim] - width, None, axis...  13.9 us
    ppermute x8, starting transfers between devices, padded(): lax.ppermute(lax.slice_in_dim(block, 0, width, axis=dim), axis, backward)  9.21 us
    ppermute x8, waiting for transfers between devices, padded(): lax.ppermute(lax.slice_in_dim(block, 0, width, axis=dim), axis, backward)  6.48 us
    concatenate x3, other arithmetic, padded(): block = jnp.concatenate([low, block, high], axis=dim)  6.44 us
  transfers between devices with their start and end apart: 19, of which 8 were waited for; matrix products, arithmetic and copies ran while one was open for 19% of the time, Pallas kernels for 0%

commit v1 on v0

--- a/solution.py
+++ b/solution.py
@@ -187,7 +187,17 @@
         zonal_flow_value, meridional_flow_value, free_top_height = ocean_step(
             zonal_flow_value, meridional_flow_value, free_top_height, wet_own, coriolis
         )
-    velocity = lax.all_gather(jnp.stack([east_start, north_start]), "trc", axis=1, tiled=True)
+    array = jnp.stack([east_start, north_start])
+    ways, here, step = (lax.axis_size("trc"), lax.axis_index("trc"), array.shape[1])
+    dims = [n * ways if d == 1 else n for d, n in enumerate(array.shape)]
+    velocity = lax.dynamic_update_slice_in_dim(
+        jnp.zeros(dims, array.dtype), array, here * step, axis=1
+    )
+    for far in range(1, ways):
+        array = lax.ppermute(array, "trc", [(d, (d + 1) % ways) for d in range(ways)])
+        velocity = lax.dynamic_update_slice_in_dim(
+            velocity, array, (here - far) % ways * step, axis=1
+        )
     flow = jnp.concatenate([velocity, wet_all[None]], 0)
     flow_ext = widen_flow(flow, 4)
     first = transport(

time: 209 us -> 213 us (1.019)
  blocking collectives: 60 us -> 44.4 us
  waiting for transfers between devices: 26 us -> 36.4 us
  starting transfers between devices: 35.1 us -> 39.6 us
  other arithmetic: 45.3 us -> 48.1 us
    all_gather x1 -> x0, blocking collectives: 15.7 us -> none  [body(): lax.all_gather(jnp.stack([east_start, north_start]), 'trc', axis=1, tiled...]
    ppermute x0 -> x3, starting transfers between devices: none -> 6.1 us  [body(): lax.ppermute(array, 'trc', [(d, (d + 1) % ways) for d in range(ways)])]
    ppermute x8, waiting for transfers between devices: 6.48 us -> 11.9 us  [padded(): lax.ppermute(lax.slice_in_dim(block, 0, width, axis=dim), axis, backward)]
    ppermute x0 -> x3, waiting for transfers between devices: none -> 4.92 us  [body(): lax.ppermute(array, 'trc', [(d, (d + 1) % ways) for d in range(ways)])]
    mul x4, other arithmetic: 18.3 us -> 22.6 us  [face_flux(): return courant * jnp.where(courant >= 0, upwind_pos, upwind_neg)]
    concatenate x3 -> x2, other arithmetic: 6.44 us -> 4.38 us  [padded(): block = jnp.concatenate([low, block, high], axis=dim)]
  transfers between devices with their start and end apart: 19 -> 22, of which waited for: 8 -> 11; matrix products, arithmetic and copies ran while one was open for 19% -> 11% of each run, Pallas kernels for 0% -> 0%
where the time goes in v1:
time: 213 us; the launch traced here: 212 us
  other arithmetic  48.1 us (23%)
  blocking collectives  44.4 us (21%)
  local copies, waits for them, and re-layouts  39.7 us (19%)
  starting transfers between devices  39.6 us (19%)
  waiting for transfers between devices  36.4 us (17%)
    psum x2, blocking collectives, ocean_step(): divergence = lax.psum(partial_div, 'trc')  44.4 us
    mul x4, other arithmetic, face_flux(): return courant * jnp.where(courant >= 0, upwind_pos, upwind_neg)  22.6 us
    ppermute x8, waiting for transfers between devices, padded(): lax.ppermute(lax.slice_in_dim(block, block.shape[dim] - width, None, axis...  16.9 us
    ppermute x8, starting transfers between devices, padded(): lax.ppermute(lax.slice_in_dim(block, block.shape[dim] - width, None, axis...  13.6 us
    ppermute x8, waiting for transfers between devices, padded(): lax.ppermute(lax.slice_in_dim(block, 0, width, axis=dim), axis, backward)  11.9 us
    ppermute x8, starting transfers between devices, padded(): lax.ppermute(lax.slice_in_dim(block, 0, width, axis=dim), axis, backward)  9.47 us
    mul x4, local copies, waits for them, and re-layouts, face_flux(): 0.5 * (1.0 - courant) * limited_slope(after - center, center - before)  7.62 us
    sub x2, other arithmetic, transport(): field[..., rows, cols] - (flux_x[..., 1:] - flux_x[..., :-1])  6.67 us
  transfers between devices with their start and end apart: 22, of which 11 were waited for; matrix products, arithmetic and copies ran while one was open for 11% of the time, Pallas kernels for 0%

profile of v1, /device:TPU:0, one launch (start us, length us, event | category | flops | bytes accessed | tf_op | source)
XLA Modules:
  0.0 211.7 jit_solution(5497111183337102706)
XLA Ops:
  3.1 3.0 %collective-permute-start = (f32[8,8,4,128]{3,1,2,0:T(8,128)S(1)}, f32[8,8,4,128]{3,1,2,0:T(8,128)S(1)}, u32[]{:S(2)}, u32[]{:S(2)}) collective-permute-start(f32[8,8,4,128]{3,1,2,0:T(8,128)S(1)} %copy.158), channel_id=1, source_target_pairs={{0,2},{2,4},{4,6},{1,3},{3,5},{5,7},{8,10},{10,12},{12,14},{9,11},... | collective-permute-start | bytes 393224 | tf_op jit(solution)/shard_map/ppermute | solution.py:28
  7.7 3.1 %collective-permute-start.4 = (f32[2,2,32,128]{3,2,1,0:T(8,128)S(1)}, f32[2,2,32,128]{3,2,1,0:T(8,128)S(1)}, u32[]{:S(2)}, u32[]{:S(2)}) collective-permute-start(f32[2,2,32,128]{3,2,1,0:T(8,128)S(1)} %get-tuple-element.51), channel_id=1, source_target_pairs={{0,8},{8,16},{16,24},{24,0},{1,9},{9,17},{17,25},{25,1},{2,10},{10... | collective-permute-start | bytes 196616 | tf_op jit(solution)/shard_map/ppermute | solution.py:197
  11.5 3.7 %copy.129 = f32[8,8,32,128]{2,1,3,0:T(8,128)} copy(f32[8,8,32,128]{3,2,1,0:T(8,128)} %param.9) | data formatting | bytes 2097152 | tf_op args[0]
  16.8 2.7 %copy.130 = f32[8,8,4,128]{2,1,3,0:T(8,128)} copy(f32[8,8,4,128]{3,1,2,0:T(8,128)S(1)} %collective-permute-done.1) | data formatting | bytes 262144 | tf_op jit(solution)/shard_map/ppermute | solution.py:31
  19.5 2.8 %copy.128 = f32[8,8,4,128]{2,1,3,0:T(8,128)} copy(f32[8,8,4,128]{3,1,2,0:T(8,128)S(1)} %collective-permute-done) | data formatting | bytes 262144 | tf_op jit(solution)/shard_map/ppermute | solution.py:28
  23.9 4.8 %collective-permute-done.6 = f32[2,2,32,128]{3,2,1,0:T(8,128)S(1)} collective-permute-done((f32[2,2,32,128]{3,2,1,0:T(8,128)S(1)}, f32[2,2,32,128]{3,2,1,0:T(8,128)S(1)}, u32[]{:S(2)}, u32[]{:S(2)}) %collective-permute-start.6) | collective-permute-done | bytes 65568 | tf_op jit(solution)/shard_map/ppermute | solution.py:197
  35.7 2.3 %collective-permute-done.8 = f32[3,8,4,128]{3,1,2,0:T(8,128)S(1)} collective-permute-done((f32[3,8,4,128]{3,1,2,0:T(8,128)S(1)}, f32[3,8,4,128]{3,1,2,0:T(8,128)S(1)}, u32[]{:S(2)}, u32[]{:S(2)}) %collective-permute-start.8) | collective-permute-done | bytes 49184 | tf_op jit(solution)/shard_map/ppermute | solution.py:31
  40.5 3.9 %pad_maximum_fusion = f32[8,8,40,136]{2,1,3,0:T(8,128)} fusion(f32[8,8,40,4]{2,1,3,0:T(8,128)S(1)} %collective-permute-done.3, f32[8,8,4,128]{2,1,3,0:T(8,128)S(1)} %copy-done.2, f32[8,8,32,128]{2,1,3,0:T(8,128)S(1)} %copy-done.1, f32[8,8,4,128]{2,1,3,0:T(8,128)S(1)} %copy-done.3, f32[8,8,40,4]{2,1,3,0:T(8,128)S(1)} %collective-permute-done.2), kind=kLoop, calls=%fused_computation.8 | loop fusion | flops 1392640 | bytes 2785280 | tf_op jit(solution)/shard_map/concatenate | solution.py:32
  44.4 6.1 %collective-permute-done.10 = f32[3,8,40,4]{3,1,2,0:T(8,128)S(1)} collective-permute-done((f32[3,8,40,4]{3,1,2,0:T(8,128)S(1)}, f32[3,8,40,4]{3,1,2,0:T(8,128)S(1)}, u32[]{:S(2)}, u32[]{:S(2)}) %collective-permute-start.10) | collective-permute-done | bytes 15392 | tf_op jit(solution)/shard_map/ppermute | solution.py:31
  50.5 10.5 %collective-permute-done.9 = f32[3,8,40,4]{3,1,2,0:T(8,128)S(1)} collective-permute-done((f32[3,8,40,4]{3,1,2,0:T(8,128)S(1)}, f32[3,8,40,4]{3,1,2,0:T(8,128)S(1)}, u32[]{:S(2)}, u32[]{:S(2)}) %collective-permute-start.9) | collective-permute-done | bytes 15392 | tf_op jit(solution)/shard_map/ppermute | solution.py:28
  72.9 2.1 %copy.140 = f32[8,37,132]{1,0,2:T(8,128)} copy(f32[8,37,132]{2,0,1:T(8,128)} %get-tuple-element.27) | data formatting | bytes 312576 | tf_op jit(solution)/shard_map/mul | solution.py:45
  80.2 1.9 copy.149
  82.1 2.0 copy.148
  86.9 2.2 %copy.144 = f32[8,32,129]{1,0,2:T(8,128)} copy(f32[8,32,129]{2,0,1:T(8,128)} %get-tuple-element.31) | data formatting | bytes 264192 | tf_op jit(solution)/shard_map/mul | solution.py:45
  90.1 8.8 %fusion.12 = f32[8,8,37,132]{2,1,3,0:T(8,128)S(1)} fusion(f32[8,8,40,136]{2,1,3,0:T(8,128)} %pad_maximum_fusion, f32[8,37,132]{1,0,2:T(8,128)S(1)} %copy.141, f32[8,37,132]{1,0,2:T(8,128)} %copy.140, f32[8,37,132]{1,0,2:T(8,128)S(1)} %copy.138, pred[8,37,132]{1,0,2:T(8,128)(4,1)} %copy.139), kind=kLoop, calls=%fused_computation.26 | loop fusion | flops 8126976 | bytes 6759456 | tf_op jit(solution)/shard_map/mul | solution.py:47
  98.9 4.9 %fusion.4 = f32[8,8,36,133]{2,1,3,0:T(8,128)S(1)} fusion(f32[8,8,40,136]{2,1,3,0:T(8,128)S(1)} %bitcast.68, f32[8,36,133]{1,0,2:T(8,128)S(1)} %copy.137, f32[8,36,133]{1,0,2:T(8,128)S(1)} %copy.136, f32[8,36,133]{1,0,2:T(8,128)S(1)} %copy.134, pred[8,36,133]{1,0,2:T(8,128)(4,1)S(1)} %copy.135), kind=kLoop, calls=%fused_computation.13 | loop fusion | flops 7967232 | bytes 6626592 | tf_op jit(solution)/shard_map/mul | solution.py:47
  103.9 2.9 %fusion.16 = f32[8,8,36,132]{2,1,3,0:T(8,128)S(1)} fusion(f32[8,8,37,132]{2,1,3,0:T(8,128)S(1)} %fusion.12, f32[8,8,36,133]{2,1,3,0:T(8,128)S(1)} %fusion.4, f32[8,8,40,136]{2,1,3,0:T(8,128)S(1)} %bitcast.68), kind=kLoop, calls=%fused_computation.31 | loop fusion | flops 1216512 | bytes 7299072 | tf_op jit(solution)/shard_map/sub | solution.py:75
  106.8 4.2 %fusion.30 = f32[8,8,33,128]{2,1,3,0:T(8,128)S(1)} fusion(f32[8,8,36,132]{2,1,3,0:T(8,128)S(1)} %fusion.16, f32[8,33,128]{1,0,2:T(8,128)S(1)} %copy-done.8, f32[8,33,128]{1,0,2:T(8,128)S(1)} %copy-done.9, f32[8,33,128]{1,0,2:T(8,128)S(1)} %copy-done.7, pred[8,33,128]{1,0,2:T(8,128)(4,1)S(1)} %copy-done.13), kind=kLoop, calls=%fused_computation.56 | loop fusion | flops 7028736 | bytes 5846016 | tf_op jit(solution)/shard_map/mul | solution.py:47
  111.1 4.7 %fusion.22 = f32[8,8,32,129]{2,1,3,0:T(8,128)S(1)} fusion(f32[8,8,36,132]{2,1,3,0:T(8,128)S(1)} %fusion.16, f32[8,32,129]{1,0,2:T(8,128)S(1)} %copy-done.5, f32[8,32,129]{1,0,2:T(8,128)S(1)} %copy-done.6, f32[8,32,129]{1,0,2:T(8,128)S(1)} %copy-done.4, pred[8,32,129]{1,0,2:T(8,128)(4,1)S(1)} %copy-done.12), kind=kLoop, calls=%fused_computation.43 | loop fusion | flops 6868992 | bytes 5713152 | tf_op jit(solution)/shard_map/mul | solution.py:47
  115.8 3.8 %fusion.34 = f32[8,8,32,128]{2,1,3,0:T(8,128)} fusion(f32[8,8,33,128]{2,1,3,0:T(8,128)S(1)} %fusion.30, f32[8,8,32,129]{2,1,3,0:T(8,128)S(1)} %fusion.22, f32[8,8,36,132]{2,1,3,0:T(8,128)S(1)} %fusion.16), kind=kLoop, calls=%fused_computation.61 | loop fusion | flops 1048576 | bytes 6291456 | tf_op jit(solution)/shard_map/sub | solution.py:75
  119.6 3.9 %copy.150 = f32[8,8,32,128]{3,1,0,2:T(8,128)} copy(f32[8,8,32,128]{2,1,3,0:T(8,128)} %fusion.34) | data formatting | bytes 2097152 | tf_op jit(solution)/shard_map/sub | solution.py:75
  123.6 3.5 %all-to-all-start = ((f32[8,8,32,128]{3,1,0,2:T(8,128)}), f32[8,8,32,128]{3,1,0,2:T(8,128)S(1)}, u32[]{:S(2)}, u32[]{:S(2)}) async-start(f32[8,8,32,128]{3,1,0,2:T(8,128)} %copy.150), calls=%async_computation | async-start | bytes 2097152 | tf_op jit(solution)/shard_map/all_to_all | solution.py:209
  127.1 3.5 %collective-permute-start.14 = (f32[5,1,128]{2,1,0:T(1,128)S(1)}, f32[5,1,128]{2,1,0:T(1,128)S(1)}, u32[]{:S(2)}, u32[]{:S(2)}) collective-permute-start(f32[5,1,128]{2,1,0:T(1,128)S(1)} %get-tuple-element.50), channel_id=1, source_target_pairs={{0,2},{2,4},{4,6},{1,3},{3,5},{5,7},{8,10},{10,12},{12,14},{9,11},... | collective-permute-start | bytes 7688 | tf_op jit(solution)/shard_map/ppermute | solution.py:28
  134.3 3.0 %collective-permute-done.12 = f32[5,32,1]{2,1,0:T(8,128)S(1)} collective-permute-done((f32[5,32,1]{2,1,0:T(8,128)S(1)}, f32[5,32,1]{2,1,0:T(8,128)S(1)}, u32[]{:S(2)}, u32[]{:S(2)}) %collective-permute-start.12) | collective-permute-done | bytes 672 | tf_op jit(solution)/shard_map/ppermute | solution.py:28
  137.3 1.8 collective-permute-done.11
  139.2 22.9 %psum.14 = f32[32,128]{1,0:T(8,128)S(1)} all-reduce(f32[32,128]{1,0:T(8,128)S(1)} %multiply_reduce_fusion.1), channel_id=1, replica_groups=mesh['trc'=4,'lat'=4,'lon'=2] {'trc'}, use_global_device_ids=true, to_apply=%region_2.0 | all-reduce | flops 4096 | bytes 32768 | tf_op jit(solution)/shard_map/psum | solution.py:135
  163.9 3.4 %all-to-all-start.2 = ((f32[8,8,128]{2,1,0:T(8,128)}), f32[8,8,128]{2,1,0:T(8,128)S(1)}, u32[]{:S(2)}, u32[]{:S(2)}) async-start(f32[8,8,128]{2,1,0:T(8,128)} %get-tuple-element.35), calls=%async_computation.2 | async-start | bytes 65536 | tf_op jit(solution)/shard_map/all_to_all | solution.py:221
  170.2 2.7 %all-to-all-done.2 = f32[8,8,128]{2,1,0:T(8,128)S(1)} async-done(((f32[8,8,128]{2,1,0:T(8,128)}), f32[8,8,128]{2,1,0:T(8,128)S(1)}, u32[]{:S(2)}, u32[]{:S(2)}) %all-to-all-start.2) | async-done | bytes 32800 | tf_op jit(solution)/shard_map/all_to_all | solution.py:221
  172.9 3.5 %all-to-all-start.1 = ((f32[32,8,8,128]{3,2,1,0:T(8,128)}), f32[32,8,8,128]{3,2,1,0:T(8,128)S(1)}, u32[]{:S(2)}, u32[]{:S(2)}) async-start(f32[32,8,8,128]{3,2,1,0:T(8,128)} %copy.152), calls=%async_computation.1 | async-start | bytes 2097152 | tf_op jit(solution)/shard_map/all_to_all | solution.py:218
  181.2 3.1 %collective-permute-done.16 = f32[5,32,1]{2,1,0:T(8,128)S(1)} collective-permute-done((f32[5,32,1]{2,1,0:T(8,128)S(1)}, f32[5,32,1]{2,1,0:T(8,128)S(1)}, u32[]{:S(2)}, u32[]{:S(2)}) %collective-permute-start.16) | collective-permute-done | bytes 672 | tf_op jit(solution)/shard_map/ppermute | solution.py:28
  184.4 1.8 collective-permute-done.15
  186.2 21.6 %psum.15 = f32[32,128]{1,0:T(8,128)S(1)} all-reduce(f32[32,128]{1,0:T(8,128)S(1)} %multiply_reduce_fusion), channel_id=1, replica_groups=mesh['trc'=4,'lat'=4,'lon'=2] {'trc'}, use_global_device_ids=true, to_apply=%region_4.5 | all-reduce | flops 4096 | bytes 32768 | tf_op jit(solution)/shard_map/psum | solution.py:135
  (138 shorter events, 55.4 us)
Async XLA Ops:
  0.6 166.6 %copy-start = (f32[32,32]{1,0:T(8,128)S(1)}, f32[32,32]{1,0:T(8,128)}, u32[]{:S(2)}) copy-start(f32[32,32]{1,0:T(8,128)} %param.15) | copy-start | bytes 12292
  1.8 15.0 %collective-permute-start.1 = (f32[8,8,4,128]{3,1,2,0:T(8,128)S(1)}, f32[8,8,4,128]{3,1,2,0:T(8,128)S(1)}, u32[]{:S(2)}, u32[]{:S(2)}) collective-permute-start(f32[8,8,4,128]{3,1,2,0:T(8,128)S(1)} %copy.159), channel_id=1, source_target_pairs={{2,0},{4,2},{6,4},{3,1},{5,3},{7,5},{10,8},{12,10},{14,12},{11,9},... | collective-permute-start | bytes 393224 | tf_op jit(solution)/shard_map/ppermute | solution.py:31
  3.1 16.4 %collective-permute-start = (f32[8,8,4,128]{3,1,2,0:T(8,128)S(1)}, f32[8,8,4,128]{3,1,2,0:T(8,128)S(1)}, u32[]{:S(2)}, u32[]{:S(2)}) collective-permute-start(f32[8,8,4,128]{3,1,2,0:T(8,128)S(1)} %copy.158), channel_id=1, source_target_pairs={{0,2},{2,4},{4,6},{1,3},{3,5},{5,7},{8,10},{10,12},{12,14},{9,11},... | collective-permute-start | bytes 393224 | tf_op jit(solution)/shard_map/ppermute | solution.py:28
  7.7 7.7 %collective-permute-start.4 = (f32[2,2,32,128]{3,2,1,0:T(8,128)S(1)}, f32[2,2,32,128]{3,2,1,0:T(8,128)S(1)}, u32[]{:S(2)}, u32[]{:S(2)}) collective-permute-start(f32[2,2,32,128]{3,2,1,0:T(8,128)S(1)} %get-tuple-element.51), channel_id=1, source_target_pairs={{0,8},{8,16},{16,24},{24,0},{1,9},{9,17},{17,25},{25,1},{2,10},{10... | collective-permute-start | bytes 196616 | tf_op jit(solution)/shard_map/ppermute | solution.py:197
  15.4 6.9 %collective-permute-start.5 = (f32[2,2,32,128]{3,2,1,0:T(8,128)S(1)}, f32[2,2,32,128]{3,2,1,0:T(8,128)S(1)}, u32[]{:S(2)}, u32[]{:S(2)}) collective-permute-start(f32[2,2,32,128]{3,2,1,0:T(8,128)S(1)} %collective-permute-done.4), channel_id=1, source_target_pairs={{0,8},{8,16},{16,24},{24,0},{1,9},{9,17},{17,25},{25,1},{2,10},{10... | collective-permute-start | bytes 196616 | tf_op jit(solution)/shard_map/ppermute | solution.py:197
  22.3 6.3 %collective-permute-start.6 = (f32[2,2,32,128]{3,2,1,0:T(8,128)S(1)}, f32[2,2,32,128]{3,2,1,0:T(8,128)S(1)}, u32[]{:S(2)}, u32[]{:S(2)}) collective-permute-start(f32[2,2,32,128]{3,2,1,0:T(8,128)S(1)} %collective-permute-done.5), channel_id=1, source_target_pairs={{0,8},{8,16},{16,24},{24,0},{1,9},{9,17},{17,25},{25,1},{2,10},{10... | collective-permute-start | bytes 196616 | tf_op jit(solution)/shard_map/ppermute | solution.py:197
  28.7 6.7 %collective-permute-start.7 = (f32[3,8,4,128]{3,1,2,0:T(8,128)S(1)}, f32[3,8,4,128]{3,1,2,0:T(8,128)S(1)}, u32[]{:S(2)}, u32[]{:S(2)}) collective-permute-start(f32[3,8,4,128]{3,1,2,0:T(8,128)S(1)} %copy.171), channel_id=1, source_target_pairs={{0,2},{2,4},{4,6},{1,3},{3,5},{5,7},{8,10},{10,12},{12,14},{9,11},... | collective-permute-start | bytes 147464 | tf_op jit(solution)/shard_map/ppermute | solution.py:28
  30.3 10.2 %copy-start.1 = (f32[8,8,32,128]{2,1,3,0:T(8,128)S(1)}, f32[8,8,32,128]{2,1,3,0:T(8,128)}, u32[]{:S(2)}) copy-start(f32[8,8,32,128]{2,1,3,0:T(8,128)} %copy.129) | copy-start | bytes 3145732
  30.3 10.2 %copy-start.2 = (f32[8,8,4,128]{2,1,3,0:T(8,128)S(1)}, f32[8,8,4,128]{2,1,3,0:T(8,128)}, u32[]{:S(2)}) copy-start(f32[8,8,4,128]{2,1,3,0:T(8,128)} %copy.130) | copy-start | bytes 393220
  30.3 10.2 %copy-start.3 = (f32[8,8,4,128]{2,1,3,0:T(8,128)S(1)}, f32[8,8,4,128]{2,1,3,0:T(8,128)}, u32[]{:S(2)}) copy-start(f32[8,8,4,128]{2,1,3,0:T(8,128)} %copy.128) | copy-start | bytes 393220
  31.9 8.3 %collective-permute-start.3 = (f32[8,8,40,4]{2,1,3,0:T(8,128)S(1)}, f32[8,8,40,4]{2,1,3,0:T(8,128)S(1)}, u32[]{:S(2)}, u32[]{:S(2)}) collective-permute-start(f32[8,8,40,4]{2,1,3,0:T(8,128)S(1)} %get-tuple-element.14), channel_id=1, source_target_pairs={{1,0},{0,1},{3,2},{2,3},{5,4},{4,5},{7,6},{6,7},{9,8},{8,9},{11,10... | collective-permute-start | bytes 122888 | tf_op jit(solution)/shard_map/ppermute | solution.py:31
  33.5 7.0 %collective-permute-start.2 = (f32[8,8,40,4]{2,1,3,0:T(8,128)S(1)}, f32[8,8,40,4]{2,1,3,0:T(8,128)S(1)}, u32[]{:S(2)}, u32[]{:S(2)}) collective-permute-start(f32[8,8,40,4]{2,1,3,0:T(8,128)S(1)} %get-tuple-element.13), channel_id=1, source_target_pairs={{0,1},{1,0},{2,3},{3,2},{4,5},{5,4},{6,7},{7,6},{8,9},{9,8},{10,11... | collective-permute-start | bytes 122888 | tf_op jit(solution)/shard_map/ppermute | solution.py:28
  34.0 4.0 %collective-permute-start.8 = (f32[3,8,4,128]{3,1,2,0:T(8,128)S(1)}, f32[3,8,4,128]{3,1,2,0:T(8,128)S(1)}, u32[]{:S(2)}, u32[]{:S(2)}) collective-permute-start(f32[3,8,4,128]{3,1,2,0:T(8,128)S(1)} %copy.172), channel_id=1, source_target_pairs={{2,0},{4,2},{6,4},{3,1},{5,3},{7,5},{10,8},{12,10},{14,12},{11,9},... | collective-permute-start | bytes 147464 | tf_op jit(solution)/shard_map/ppermute | solution.py:31
  38.2 12.3 %collective-permute-start.10 = (f32[3,8,40,4]{3,1,2,0:T(8,128)S(1)}, f32[3,8,40,4]{3,1,2,0:T(8,128)S(1)}, u32[]{:S(2)}, u32[]{:S(2)}) collective-permute-start(f32[3,8,40,4]{3,1,2,0:T(8,128)S(1)} %get-tuple-element.24), channel_id=1, source_target_pairs={{1,0},{0,1},{3,2},{2,3},{5,4},{4,5},{7,6},{6,7},{9,8},{8,9},{11,10... | collective-permute-start | bytes 46088 | tf_op jit(solution)/shard_map/ppermute | solution.py:31
  39.7 21.3 %collective-permute-start.9 = (f32[3,8,40,4]{3,1,2,0:T(8,128)S(1)}, f32[3,8,40,4]{3,1,2,0:T(8,128)S(1)}, u32[]{:S(2)}, u32[]{:S(2)}) collective-permute-start(f32[3,8,40,4]{3,1,2,0:T(8,128)S(1)} %get-tuple-element.23), channel_id=1, source_target_pairs={{0,1},{1,0},{2,3},{3,2},{4,5},{5,4},{6,7},{7,6},{8,9},{9,8},{10,11... | collective-permute-start | bytes 46088 | tf_op jit(solution)/shard_map/ppermute | solution.py:28
  69.4 19.6 %copy-start.14 = (pred[8,32,129]{2,0,1:T(8,128)(4,1)S(1)}, pred[8,32,129]{2,0,1:T(8,128)(4,1)}, u32[]{:S(2)}) copy-start(pred[8,32,129]{2,0,1:T(8,128)(4,1)} %get-tuple-element.5) | copy-start | bytes 99076
  71.5 14.2 %copy-start.10 = (f32[8,32,129]{2,0,1:T(8,128)S(1)}, f32[8,32,129]{2,0,1:T(8,128)}, u32[]{:S(2)}) copy-start(f32[8,32,129]{2,0,1:T(8,128)} %get-tuple-element.32) | copy-start | bytes 396292
  86.9 12.0 %slice-start = ((s8[4456448]{0:T(1024)(128)(4,1)}), s8[262144]{0:T(1024)(128)(4,1)S(1)}, s32[]{:S(2)}) async-start(s8[4456448]{0:T(1024)(128)(4,1)} %bitcast.67), calls=%async_computation.3 | async-start | bytes 524288
  119.6 42.8 %copy-start.16 = (f32[32]{0:T(128)S(1)}, f32[32]{0:T(128)}, u32[]{:S(2)}) copy-start(f32[32]{0:T(128)} %param.17) | copy-start | bytes 388
  119.6 47.7 %copy-start.17 = (f32[32]{0:T(128)S(1)}, f32[32]{0:T(128)}, u32[]{:S(2)}) copy-start(f32[32]{0:T(128)} %param.16) | copy-start | bytes 388
  123.6 38.8 %all-to-all-start = ((f32[8,8,32,128]{3,1,0,2:T(8,128)}), f32[8,8,32,128]{3,1,0,2:T(8,128)S(1)}, u32[]{:S(2)}, u32[]{:S(2)}) async-start(f32[8,8,32,128]{3,1,0,2:T(8,128)} %copy.150), calls=%async_computation | async-start | bytes 2097152 | tf_op jit(solution)/shard_map/all_to_all | solution.py:209
  127.1 11.9 %collective-permute-start.14 = (f32[5,1,128]{2,1,0:T(1,128)S(1)}, f32[5,1,128]{2,1,0:T(1,128)S(1)}, u32[]{:S(2)}, u32[]{:S(2)}) collective-permute-start(f32[5,1,128]{2,1,0:T(1,128)S(1)} %get-tuple-element.50), channel_id=1, source_target_pairs={{0,2},{2,4},{4,6},{1,3},{3,5},{5,7},{8,10},{10,12},{12,14},{9,11},... | collective-permute-start | bytes 7688 | tf_op jit(solution)/shard_map/ppermute | solution.py:28
  130.7 8.4 %collective-permute-start.13 = (f32[5,1,128]{2,1,0:T(1,128)S(1)}, f32[5,1,128]{2,1,0:T(1,128)S(1)}, u32[]{:S(2)}, u32[]{:S(2)}) collective-permute-start(f32[5,1,128]{2,1,0:T(1,128)S(1)} %get-tuple-element.49), channel_id=1, source_target_pairs={{2,0},{4,2},{6,4},{3,1},{5,3},{7,5},{10,8},{12,10},{14,12},{11,9},... | collective-permute-start | bytes 7688 | tf_op jit(solution)/shard_map/ppermute | solution.py:31
  132.1 5.2 %collective-permute-start.12 = (f32[5,32,1]{2,1,0:T(8,128)S(1)}, f32[5,32,1]{2,1,0:T(8,128)S(1)}, u32[]{:S(2)}, u32[]{:S(2)}) collective-permute-start(f32[5,32,1]{2,1,0:T(8,128)S(1)} %get-tuple-element.48), channel_id=1, source_target_pairs={{0,1},{1,0},{2,3},{3,2},{4,5},{5,4},{6,7},{7,6},{8,9},{9,8},{10,11... | collective-permute-start | bytes 1928 | tf_op jit(solution)/shard_map/ppermute | solution.py:28
  133.6 5.4 %collective-permute-start.11 = (f32[5,32,1]{2,1,0:T(8,128)S(1)}, f32[5,32,1]{2,1,0:T(8,128)S(1)}, u32[]{:S(2)}, u32[]{:S(2)}) collective-permute-start(f32[5,32,1]{2,1,0:T(8,128)S(1)} %get-tuple-element.47), channel_id=1, source_target_pairs={{1,0},{0,1},{3,2},{2,3},{5,4},{4,5},{7,6},{6,7},{9,8},{8,9},{11,10... | collective-permute-start | bytes 1928 | tf_op jit(solution)/shard_map/ppermute | solution.py:31
  163.9 46.1 %copy-start.15 = (f32[2,32,128]{2,1,0:T(8,128)S(1)}, f32[2,32,128]{2,1,0:T(8,128)}, u32[]{:S(2)}) copy-start(f32[2,32,128]{2,1,0:T(8,128)} %param.12) | copy-start | bytes 98308
  163.9 9.0 %all-to-all-start.2 = ((f32[8,8,128]{2,1,0:T(8,128)}), f32[8,8,128]{2,1,0:T(8,128)S(1)}, u32[]{:S(2)}, u32[]{:S(2)}) async-start(f32[8,8,128]{2,1,0:T(8,128)} %get-tuple-element.35), calls=%async_computation.2 | async-start | bytes 65536 | tf_op jit(solution)/shard_map/all_to_all | solution.py:221
  172.9 37.7 %all-to-all-start.1 = ((f32[32,8,8,128]{3,2,1,0:T(8,128)}), f32[32,8,8,128]{3,2,1,0:T(8,128)S(1)}, u32[]{:S(2)}, u32[]{:S(2)}) async-start(f32[32,8,8,128]{3,2,1,0:T(8,128)} %copy.152), calls=%async_computation.1 | async-start | bytes 2097152 | tf_op jit(solution)/shard_map/all_to_all | solution.py:218
  176.5 9.7 %collective-permute-start.18 = (f32[5,1,128]{2,1,0:T(1,128)S(1)}, f32[5,1,128]{2,1,0:T(1,128)S(1)}, u32[]{:S(2)}, u32[]{:S(2)}) collective-permute-start(f32[5,1,128]{2,1,0:T(1,128)S(1)} %get-tuple-element.44), channel_id=1, source_target_pairs={{0,2},{2,4},{4,6},{1,3},{3,5},{5,7},{8,10},{10,12},{12,14},{9,11},... | collective-permute-start | bytes 7688 | tf_op jit(solution)/shard_map/ppermute | solution.py:28
  177.7 8.4 %collective-permute-start.17 = (f32[5,1,128]{2,1,0:T(1,128)S(1)}, f32[5,1,128]{2,1,0:T(1,128)S(1)}, u32[]{:S(2)}, u32[]{:S(2)}) collective-permute-start(f32[5,1,128]{2,1,0:T(1,128)S(1)} %get-tuple-element.43), channel_id=1, source_target_pairs={{2,0},{4,2},{6,4},{3,1},{5,3},{7,5},{10,8},{12,10},{14,12},{11,9},... | collective-permute-start | bytes 7688 | tf_op jit(solution)/shard_map/ppermute | solution.py:31
  179.2 5.2 %collective-permute-start.16 = (f32[5,32,1]{2,1,0:T(8,128)S(1)}, f32[5,32,1]{2,1,0:T(8,128)S(1)}, u32[]{:S(2)}, u32[]{:S(2)}) collective-permute-start(f32[5,32,1]{2,1,0:T(8,128)S(1)} %get-tuple-element.42), channel_id=1, source_target_pairs={{0,1},{1,0},{2,3},{3,2},{4,5},{5,4},{6,7},{7,6},{8,9},{9,8},{10,11... | collective-permute-start | bytes 1928 | tf_op jit(solution)/shard_map/ppermute | solution.py:28
  180.7 5.4 %collective-permute-start.15 = (f32[5,32,1]{2,1,0:T(8,128)S(1)}, f32[5,32,1]{2,1,0:T(8,128)S(1)}, u32[]{:S(2)}, u32[]{:S(2)}) collective-permute-start(f32[5,32,1]{2,1,0:T(8,128)S(1)} %get-tuple-element.41), channel_id=1, source_target_pairs={{1,0},{0,1},{3,2},{2,3},{5,4},{4,5},{7,6},{6,7},{9,8},{8,9},{11,10... | collective-permute-start | bytes 1928 | tf_op jit(solution)/shard_map/ppermute | solution.py:31
  (10 other events, 45.0 us)
